TPU v7x, 32 devices: a whole 2x2x4 slice. The times are simulated.
32 devices in a mesh: sector: 16 (over z, y, x), op: 2 (over core).
Axes of the slice: x: 2, y: 2, z: 4, core: 2. Of those that a mesh axis runs over, the one named last changes fastest.
Arguments:
- wave_start: float32 [32, 256, 256], P('sector'), may hold values from -6 to 6
- left_blocks: float32 [4, 32, 256, 256], P('op', 'sector'), may hold values from -0.375 to 0.375
- right_blocks: float32 [4, 32, 256, 256], P('op', 'sector'), may hold values from -0.1875 to 0.1875
- term_shifts: int32 [4], P('op'), may hold values from -1 to 1
- preconditioner: float32 [32, 256, 256], P('sector'), may hold values from 0.5 to 4
Outputs:
- basis: float32 [3, 32, 256, 256], P(None, 'sector', 'op')
- ritz: float32 [3], replicated
Inputs may be any that keep to these rules, and one draw needn't show every extreme that they name: Each term changes the charge sector by term_shifts, one of -1, 0 and 1.
All inputs are finite; a program needn't handle non-finite values.
Results may differ from a plain program's by a relative error of at most 0.0003.
Values sent between devices are 32-bit elements; how exact they have to be, the bound alone decides.
No kernel may reach another device: no remote copies, remote signals or barrier semaphores. Data moves between devices by JAX's collectives and lax.ppermute only.
A program may use at most 64 MiB of HBM per device.

v0:
```python
import jax
import jax.numpy as jnp
from jax import lax
from jax.sharding import PartitionSpec as P

ITERS = 3
EPSILON = 1e-06


def with_halo(cells, sides, width):
    for axis, dim in sides:
        count = lax.axis_size(axis)
        ends = count - 1
        head = lax.slice_in_dim(cells, 0, width, axis=dim)
        tail = lax.slice_in_dim(cells, cells.shape[dim] - width, cells.shape[dim], axis=dim)
        cells = jnp.concatenate(
            [
                lax.ppermute(tail, axis, [(i, (i + 1) % count) for i in range(ends)]),
                cells,
                lax.ppermute(head, axis, [((i + 1) % count, i) for i in range(ends)]),
            ],
            axis=dim,
        )
    return cells


def body(wave_start, left_blocks, right_blocks, term_shifts, preconditioner):
    highest = lax.Precision.HIGHEST
    width = wave_start.shape[1]
    row_count = width // lax.axis_size("op")
    first_row = lax.axis_index("op") * row_count
    total = float(wave_start.shape[0] * lax.axis_size("sector") * width * wave_start.shape[2])

    def own_rows(values):
        return lax.dynamic_slice_in_dim(values, first_row, row_count, axis=values.ndim - 2)

    def portion(values):
        return own_rows(values)

    start_sum = lax.psum(jnp.sum(jnp.square(portion(wave_start))), ("sector", "op")) / total
    factor = lax.rsqrt(start_sum + EPSILON)
    applied = wave_start * factor
    basis = [wave_start * factor]
    ritz = []
    for index in range(ITERS):
        latest = basis[-1]
        padded = with_halo(applied, (("sector", 0),), 1)
        shift = term_shifts[:, None, None, None]
        source = jnp.where(
            shift == 1,
            padded[None, :-2],
            jnp.where(shift == -1, padded[None, 2:], padded[None, 1:-1]),
        )
        inner = jnp.einsum("ksab,ksbc->ksac", left_blocks, source, precision=highest)
        image = lax.psum(jnp.einsum("ksac,kscd->sad", inner, right_blocks, precision=highest), "op")
        ratio_image = image / preconditioner
        ratio_basis = latest / preconditioner
        part_image = portion(ratio_image)
        part_basis = portion(ratio_basis)
        pieces = [
            jnp.sum(portion(latest) * portion(image)),
            jnp.sum(part_image * part_image),
            jnp.sum(part_image * part_basis),
            jnp.sum(part_basis * part_basis),
        ]
        pieces = pieces + [jnp.sum(portion(member) * part_image) for member in basis]
        pieces = pieces + [jnp.sum(portion(member) * part_basis) for member in basis]
        sums = lax.psum(jnp.stack(pieces), ("sector", "op")) / total
        count = len(basis)
        theta = sums[0]
        correlations = sums[4 : 4 + count] - theta * sums[4 + count :]
        correction = ratio_image - theta * ratio_basis
        ortho = correction
        for position, member in enumerate(basis):
            ortho = ortho - correlations[position] * member
        length = (
            sums[1]
            - 2.0 * theta * sums[2]
            + theta * theta * sums[3]
            - jnp.sum(jnp.square(correlations))
        )
        fresh = ortho * lax.rsqrt(length + EPSILON)
        basis.append(fresh)
        ritz.append(theta)
        if index + 1 < ITERS:
            applied = fresh
    output = jnp.stack([portion(member) for member in basis[1:]])
    return (output, jnp.stack(ritz))


def solution(mesh):
    placed = (
        P("sector", None, None),
        P("op", "sector", None, None),
        P("op", "sector", None, None),
        P("op"),
        P("sector", None, None),
    )
    return jax.shard_map(
        body,
        mesh=mesh,
        in_specs=placed,
        out_specs=(P(None, "sector", "op", None), P()),
        check_vma=False,
    )
```

profile of v0, /device:TPU:0, one launch (start us, length us, event | category | flops | bytes accessed | tf_op | source)
XLA Modules:
  0.0 348.4 jit_solution(17925297234444958489)
XLA Ops:
  7.2 1.7 multiply_reduce_fusion.24
  8.9 42.2 %psum.49 = f32[]{:T(128)} all-reduce(f32[]{:T(128)} %multiply_reduce_fusion.24), channel_id=1, replica_groups=mesh['sector'=16,'op'=2] {'sector','op'}, use_global_device_ids=true, to_apply=%region_1.0 | all-reduce | flops 1 | bytes 8 | tf_op jit(solution)/shard_map/psum | solution.py:40
  53.2 4.3 %collective-permute-start = (f32[1,256,256]{2,1,0:T(8,128)S(1)}, f32[1,256,256]{2,1,0:T(8,128)S(1)}, u32[]{:S(2)}, u32[]{:S(2)}) collective-permute-start(f32[1,256,256]{2,1,0:T(8,128)S(1)} %get-tuple-element.48), channel_id=1, source_target_pairs={{0,2},{2,4},{4,6},{6,8},{8,10},{10,12},{12,14},{14,16},{16,18},{18... | collective-permute-start | bytes 786440 | tf_op jit(solution)/shard_map/ppermute | solution.py:18
  58.8 8.3 %collective-permute-done = f32[1,256,256]{2,1,0:T(8,128)S(1)} collective-permute-done((f32[1,256,256]{2,1,0:T(8,128)S(1)}, f32[1,256,256]{2,1,0:T(8,128)S(1)}, u32[]{:S(2)}, u32[]{:S(2)}) %collective-permute-start) | collective-permute-done | bytes 262176 | tf_op jit(solution)/shard_map/ppermute | solution.py:18
  67.2 1.9 collective-permute-done.1
  69.2 1.4 convolution_bitcast_fusion.2
  70.5 2.0 convolution_bitcast_fusion.5
  72.5 17.9 %all-reduce.4.cloned.1.call-done = f32[2,256,256]{2,1,0:T(8,128)} async-done(((f32[2,256,256]{2,1,0:T(8,128)}), f32[2,256,256]{2,1,0:T(8,128)}) %all-reduce.4.cloned.1.call-update) | async-done | bytes 524304 | tf_op jit(solution)/shard_map/psum | solution.py:55
  92.5 3.8 %stack.102 = f32[6]{0:T(128)S(1)} concatenate(f32[1]{0:T(128)} %bitcast.3, f32[1]{0:T(128)} %bitcast.4, f32[1]{0:T(128)} %bitcast.5, f32[1]{0:T(128)} %bitcast.6, f32[1]{0:T(128)} %bitcast.7, f32[1]{0:T(128)} %bitcast.8), dimensions={0} | concatenate | bytes 48 | tf_op jit(solution)/shard_map/stack | solution.py:68
  96.3 40.5 %psum.51 = f32[6]{0:T(128)S(1)} all-reduce(f32[6]{0:T(128)S(1)} %stack.102), channel_id=1, replica_groups=mesh['sector'=16,'op'=2] {'sector','op'}, use_global_device_ids=true, to_apply=%region_9.10 | all-reduce | flops 6 | bytes 48 | tf_op jit(solution)/shard_map/psum | solution.py:68
  143.4 2.0 fusion.10
  145.5 4.2 %collective-permute-start.2 = (f32[1,256,256]{2,1,0:T(8,128)S(1)}, f32[1,256,256]{2,1,0:T(8,128)S(1)}, u32[]{:S(2)}, u32[]{:S(2)}) collective-permute-start(f32[1,256,256]{2,1,0:T(8,128)S(1)} %get-tuple-element.44), channel_id=1, source_target_pairs={{0,2},{2,4},{4,6},{6,8},{8,10},{10,12},{12,14},{14,16},{16,18},{18... | collective-permute-start | bytes 786440 | tf_op jit(solution)/shard_map/ppermute | solution.py:18
  151.0 8.2 %collective-permute-done.2 = f32[1,256,256]{2,1,0:T(8,128)S(1)} collective-permute-done((f32[1,256,256]{2,1,0:T(8,128)S(1)}, f32[1,256,256]{2,1,0:T(8,128)S(1)}, u32[]{:S(2)}, u32[]{:S(2)}) %collective-permute-start.2) | collective-permute-done | bytes 262176 | tf_op jit(solution)/shard_map/ppermute | solution.py:18
  159.3 1.8 collective-permute-done.3
  161.2 1.4 convolution_bitcast_fusion.1
  162.5 1.9 convolution_bitcast_fusion.4
  164.5 18.0 %all-reduce.6.cloned.1.call-done = f32[2,256,256]{2,1,0:T(8,128)} async-done(((f32[2,256,256]{2,1,0:T(8,128)}), f32[2,256,256]{2,1,0:T(8,128)}) %all-reduce.6.cloned.1.call-update) | async-done | bytes 524304 | tf_op jit(solution)/shard_map/psum | solution.py:55
  184.6 5.1 %stack.112 = f32[8]{0:T(128)S(1)} concatenate(f32[1]{0:T(128)} %bitcast.19, f32[1]{0:T(128)} %bitcast.20, f32[1]{0:T(128)} %bitcast.21, f32[1]{0:T(128)} %bitcast.22, f32[1]{0:T(128)} %bitcast.23, f32[1]{0:T(128)} %bitcast.24, f32[1]{0:T(128)} %bitcast.25, f32[1]{0:T(128)} %bitcast.26), dimensions={0} | concatenate | bytes 64 | tf_op jit(solution)/shard_map/stack | solution.py:68
  189.8 40.5 %psum.53 = f32[8]{0:T(128)S(1)} all-reduce(f32[8]{0:T(128)S(1)} %stack.112), channel_id=1, replica_groups=mesh['sector'=16,'op'=2] {'sector','op'}, use_global_device_ids=true, to_apply=%region_19.20 | all-reduce | flops 8 | bytes 64 | tf_op jit(solution)/shard_map/psum | solution.py:68
  237.2 4.1 %fusion.9 = (f32[2,256,256]{2,1,0:T(8,128)}, f32[2,256,256]{2,1,0:T(8,128)S(1)}) fusion(f32[2,256,256]{2,1,0:T(8,128)S(1)} %copy-done.1, f32[]{:T(128)S(6)} %rsqrt.14, f32[2,256,256]{2,1,0:T(8,128)S(1)} %get-tuple-element.33, f32[]{:T(128)} %bitcast.29, f32[2,256,256]{2,1,0:T(8,128)S(1)} %get-tuple-element.35, f32[]{:T(128)} %bitcast.28, ...), kind=kLoop, calls=%fused_computation.66 | loop fusion | flops 1048576 | bytes 3670032 | tf_op jit(solution)/shard_map/div | solution.py:57
  241.3 4.2 %collective-permute-start.4 = (f32[1,256,256]{2,1,0:T(8,128)S(1)}, f32[1,256,256]{2,1,0:T(8,128)S(1)}, u32[]{:S(2)}, u32[]{:S(2)}) collective-permute-start(f32[1,256,256]{2,1,0:T(8,128)S(1)} %get-tuple-element.40), channel_id=1, source_target_pairs={{0,2},{2,4},{4,6},{6,8},{8,10},{10,12},{12,14},{14,16},{16,18},{18... | collective-permute-start | bytes 786440 | tf_op jit(solution)/shard_map/ppermute | solution.py:18
  245.5 1.5 collective-permute-start.5
  247.0 8.0 %collective-permute-done.4 = f32[1,256,256]{2,1,0:T(8,128)S(1)} collective-permute-done((f32[1,256,256]{2,1,0:T(8,128)S(1)}, f32[1,256,256]{2,1,0:T(8,128)S(1)}, u32[]{:S(2)}, u32[]{:S(2)}) %collective-permute-start.4) | collective-permute-done | bytes 262176 | tf_op jit(solution)/shard_map/ppermute | solution.py:18
  255.0 1.8 collective-permute-done.5
  256.9 1.4 convolution_bitcast_fusion
  258.3 1.9 convolution_bitcast_fusion.3
  260.2 18.0 %all-reduce.8.cloned.1.call-done = f32[2,256,256]{2,1,0:T(8,128)} async-done(((f32[2,256,256]{2,1,0:T(8,128)}), f32[2,256,256]{2,1,0:T(8,128)}) %all-reduce.8.cloned.1.call-update) | async-done | bytes 524304 | tf_op jit(solution)/shard_map/psum | solution.py:55
  279.6 1.5 multiply_reduce_fusion
  281.1 6.2 %stack.124 = f32[10]{0:T(128)S(1)} concatenate(f32[1]{0:T(128)} %bitcast.37, f32[1]{0:T(128)} %bitcast.38, f32[1]{0:T(128)} %bitcast.39, f32[1]{0:T(128)} %bitcast.40, f32[1]{0:T(128)} %bitcast.41, f32[1]{0:T(128)} %bitcast.42, f32[1]{0:T(128)} %bitcast.43, f32[1]{0:T(128)} %bitcast.44, f32[1]{0:T(128)} %bitcast.45, f32[1]{0:T(128)} %bitcast.46), dimensions={0} | concatenate | bytes 80 | tf_op jit(solution)/shard_map/stack | solution.py:68
  287.4 40.5 %psum.55 = f32[10]{0:T(128)S(1)} all-reduce(f32[10]{0:T(128)S(1)} %stack.124), channel_id=1, replica_groups=mesh['sector'=16,'op'=2] {'sector','op'}, use_global_device_ids=true, to_apply=%region_32.33 | all-reduce | flops 10 | bytes 80 | tf_op jit(solution)/shard_map/psum | solution.py:68
  330.5 2.5 pad_maximum_fusion.7
  337.4 3.5 %multiply_bitcast_fusion = f32[1,2,128,256]{3,2,1,0:T(8,128)S(1)} fusion(f32[2,256,256]{2,1,0:T(8,128)S(1)} %get-tuple-element.29, s32[]{:T(128)S(6)} %select_n.22, f32[2,256,256]{2,1,0:T(8,128)} %copy-done.11, f32[2,256,256]{2,1,0:T(8,128)S(1)} %copy-done.10, f32[2,256,256]{2,1,0:T(8,128)S(1)} %get-tuple-element.33, ...), kind=kLoop, calls=%fused_computation.27 | loop fusion | flops 589824 | bytes 1572888 | tf_op jit(solution)/shard_map/stack | solution.py:87
  (66 shorter events, 16.7 us)
Async XLA Ops:
  7.2 62.0 %copy-start = (f32[2,2,256,256]{3,2,1,0:T(8,128)S(1)}, f32[2,2,256,256]{3,2,1,0:T(8,128)}, u32[]{:S(2)}) copy-start(f32[2,2,256,256]{3,2,1,0:T(8,128)} %param.6) | copy-start | bytes 3145732
  7.2 83.3 %all-reduce.4.cloned.1.call-start = ((), (), s32[]{:S(2)}) async-start(), calls=%async_computation | async-start | bytes 1048576 | tf_op jit(solution)/shard_map/psum | solution.py:55
  53.1 38.6 %copy-start.6 = (f32[2,256,256]{2,1,0:T(8,128)}, f32[2,256,256]{2,1,0:T(8,128)S(1)}, u32[]{:S(2)}) copy-start(f32[2,256,256]{2,1,0:T(8,128)S(1)} %get-tuple-element.34) | copy-start | bytes 1572868
  53.2 5.6 %copy-start.16 = (s32[2]{0:T(128)S(1)}, s32[2]{0:T(128)}, u32[]{:S(2)}) copy-start(s32[2]{0:T(128)} %param.8) | copy-start | bytes 28
  53.2 14.0 %collective-permute-start = (f32[1,256,256]{2,1,0:T(8,128)S(1)}, f32[1,256,256]{2,1,0:T(8,128)S(1)}, u32[]{:S(2)}, u32[]{:S(2)}) collective-permute-start(f32[1,256,256]{2,1,0:T(8,128)S(1)} %get-tuple-element.48), channel_id=1, source_target_pairs={{0,2},{2,4},{4,6},{6,8},{8,10},{10,12},{12,14},{14,16},{16,18},{18... | collective-permute-start | bytes 786440 | tf_op jit(solution)/shard_map/ppermute | solution.py:18
  57.5 11.5 %collective-permute-start.1 = (f32[1,256,256]{2,1,0:T(8,128)S(1)}, f32[1,256,256]{2,1,0:T(8,128)S(1)}, u32[]{:S(2)}, u32[]{:S(2)}) collective-permute-start(f32[1,256,256]{2,1,0:T(8,128)S(1)} %get-tuple-element.49), channel_id=1, source_target_pairs={{2,0},{4,2},{6,4},{8,6},{10,8},{12,10},{14,12},{16,14},{18,16},{20... | collective-permute-start | bytes 786440 | tf_op jit(solution)/shard_map/ppermute | solution.py:20
  69.1 1.4 copy-start.2
  72.5 18.0 %copy-start.1 = (f32[2,256,256]{2,1,0:T(8,128)S(1)}, f32[2,256,256]{2,1,0:T(8,128)}, u32[]{:S(2)}) copy-start(f32[2,256,256]{2,1,0:T(8,128)} %param.9) | copy-start | bytes 1572868
  72.5 110.0 %all-reduce.6.cloned.1.call-start = ((), (), s32[]{:S(2)}) async-start(), calls=%async_computation.1 | async-start | bytes 1048576 | tf_op jit(solution)/shard_map/psum | solution.py:55
  90.5 1.2 copy-start.14
  91.7 0.8 copy-start.8
  145.5 38.2 %copy-start.5 = (f32[2,256,256]{2,1,0:T(8,128)}, f32[2,256,256]{2,1,0:T(8,128)S(1)}, u32[]{:S(2)}) copy-start(f32[2,256,256]{2,1,0:T(8,128)S(1)} %get-tuple-element.32) | copy-start | bytes 1572868
  145.5 13.7 %collective-permute-start.2 = (f32[1,256,256]{2,1,0:T(8,128)S(1)}, f32[1,256,256]{2,1,0:T(8,128)S(1)}, u32[]{:S(2)}, u32[]{:S(2)}) collective-permute-start(f32[1,256,256]{2,1,0:T(8,128)S(1)} %get-tuple-element.44), channel_id=1, source_target_pairs={{0,2},{2,4},{4,6},{6,8},{8,10},{10,12},{12,14},{14,16},{16,18},{18... | collective-permute-start | bytes 786440 | tf_op jit(solution)/shard_map/ppermute | solution.py:18
  149.7 11.3 %collective-permute-start.3 = (f32[1,256,256]{2,1,0:T(8,128)S(1)}, f32[1,256,256]{2,1,0:T(8,128)S(1)}, u32[]{:S(2)}, u32[]{:S(2)}) collective-permute-start(f32[1,256,256]{2,1,0:T(8,128)S(1)} %get-tuple-element.45), channel_id=1, source_target_pairs={{2,0},{4,2},{6,4},{8,6},{10,8},{12,10},{14,12},{16,14},{18,16},{20... | collective-permute-start | bytes 786440 | tf_op jit(solution)/shard_map/ppermute | solution.py:20
  161.1 1.4 copy-start.3
  164.5 113.8 %all-reduce.8.cloned.1.call-start = ((), (), s32[]{:S(2)}) async-start(), calls=%async_computation.2 | async-start | bytes 1048576 | tf_op jit(solution)/shard_map/psum | solution.py:55
  182.5 1.2 copy-start.13
  183.7 0.9 copy-start.7
  241.3 13.7 %collective-permute-start.4 = (f32[1,256,256]{2,1,0:T(8,128)S(1)}, f32[1,256,256]{2,1,0:T(8,128)S(1)}, u32[]{:S(2)}, u32[]{:S(2)}) collective-permute-start(f32[1,256,256]{2,1,0:T(8,128)S(1)} %get-tuple-element.40), channel_id=1, source_target_pairs={{0,2},{2,4},{4,6},{6,8},{8,10},{10,12},{12,14},{14,16},{16,18},{18... | collective-permute-start | bytes 786440 | tf_op jit(solution)/shard_map/ppermute | solution.py:18
  245.5 11.3 %collective-permute-start.5 = (f32[1,256,256]{2,1,0:T(8,128)S(1)}, f32[1,256,256]{2,1,0:T(8,128)S(1)}, u32[]{:S(2)}, u32[]{:S(2)}) collective-permute-start(f32[1,256,256]{2,1,0:T(8,128)S(1)} %get-tuple-element.41), channel_id=1, source_target_pairs={{2,0},{4,2},{6,4},{8,6},{10,8},{12,10},{14,12},{16,14},{18,16},{20... | collective-permute-start | bytes 786440 | tf_op jit(solution)/shard_map/ppermute | solution.py:20
  256.9 1.4 copy-start.4
  278.2 1.2 copy-start.9
  278.2 1.4 copy-start.12
  279.5 1.7 copy-start.11
  279.6 57.8 %copy-start.10 = (f32[2,256,256]{2,1,0:T(8,128)S(1)}, f32[2,256,256]{2,1,0:T(8,128)}, u32[]{:S(2)}) copy-start(f32[2,256,256]{2,1,0:T(8,128)} %get-tuple-element.28) | copy-start | bytes 1572868
  337.4 3.5 %copy-start.15 = (f32[1,2,128,256]{3,2,1,0:T(8,128)S(1)}, f32[1,2,128,256]{3,2,1,0:T(8,128)}, u32[]{:S(2)}) copy-start(f32[1,2,128,256]{3,2,1,0:T(8,128)} %get-tuple-element.37) | copy-start | bytes 786436
Sparse Core Ops, SparseCore 0:
  72.6 17.8 all-reduce.3
  164.6 17.8 all-reduce.5
  260.4 17.8 all-reduce.7
where the time goes:
time: 350 us; the launch traced here: 348 us
  blocking collectives  164 us (47%)
  waiting for transfers between devices  84 us (24%)
  between operations  29.4 us (8%)
  other arithmetic  25.7 us (7%)
  local copies, waits for them, and re-layouts  18.8 us (5%)
  starting transfers between devices  16.9 us (5%)
  matrix products  9.9 us (3%)
    psum x3, blocking collectives, body(): sums = lax.psum(jnp.stack(pieces), ('sector', 'op')) / total  122 us
    psum x3, waiting for transfers between devices, body(): lax.psum(jnp.einsum('ksac,kscd->sad', inner, right_blocks, precision=high...  53.9 us
    psum x1, blocking collectives, body(): lax.psum(jnp.sum(jnp.square(portion(wave_start))), ('sector', 'op')) / total  42.2 us
    ppermute x3, waiting for transfers between devices, with_halo(): lax.ppermute(tail, axis, [(i, (i + 1) % count) for i in range(ends)])  24.5 us
    another operation x3, local copies, waits for them, and re-layouts, body(): sums = lax.psum(jnp.stack(pieces), ('sector', 'op')) / total  15.2 us
    ppermute x3, starting transfers between devices, with_halo(): lax.ppermute(tail, axis, [(i, (i + 1) % count) for i in range(ends)])  12.7 us
    div x3, other arithmetic, body(): ratio_basis = latest / preconditioner  7.41 us
  transfers between devices with their start and end apart: 9, of which 9 were waited for; matrix products, arithmetic and copies ran while one was open for 0% of the time, Pallas kernels for 0%

commit v1 on v0

--- a/solution.py
+++ b/solution.py
@@ -52,7 +52,12 @@
             jnp.where(shift == -1, padded[None, 2:], padded[None, 1:-1]),
         )
         inner = jnp.einsum("ksab,ksbc->ksac", left_blocks, source, precision=highest)
-        image = lax.psum(jnp.einsum("ksac,kscd->sad", inner, right_blocks, precision=highest), "op")
+        image = jnp.sum(
+            lax.all_gather(
+                jnp.einsum("ksac,kscd->sad", inner, right_blocks, precision=highest), "op"
+            ),
+            axis=0,
+        )
         ratio_image = image / preconditioner
         ratio_basis = latest / preconditioner
         part_image = portion(ratio_image)

time: 350 us -> 327 us (0.934)
  waiting for transfers between devices: 84 us -> 54.9 us
  other arithmetic: 25.7 us -> 32.2 us
    psum x3 -> x0, waiting for transfers between devices: 53.9 us -> none  [body(): lax.psum(jnp.einsum('ksac,kscd->sad', inner, right_blocks, precision=high...]
    all_gather x0 -> x3, waiting for transfers between devices: none -> 24.8 us  [body(): lax.all_gather(jnp.einsum('ksac,kscd->sad', inner, right_blocks, precisio...]
    reduce_sum x0 -> x3, other arithmetic: none -> 6.5 us  [body(): jnp.sum(lax.all_gather(jnp.einsum('ksac,kscd->sad', inner, right_blocks,...]
where the time goes in v1:
time: 327 us; the launch traced here: 326 us
  blocking collectives  164 us (50%)
  waiting for transfers between devices  54.9 us (17%)
  other arithmetic  32.2 us (10%)
  between operations  29.3 us (9%)
  local copies, waits for them, and re-layouts  18.9 us (6%)
  starting transfers between devices  16.9 us (5%)
  matrix products  9.93 us (3%)
    psum x3, blocking collectives, body(): sums = lax.psum(jnp.stack(pieces), ('sector', 'op')) / total  121 us
    psum x1, blocking collectives, body(): lax.psum(jnp.sum(jnp.square(portion(wave_start))), ('sector', 'op')) / total  42.2 us
    all_gather x3, waiting for transfers between devices, body(): lax.all_gather(jnp.einsum('ksac,kscd->sad', inner, right_blocks, precisio...  24.8 us
    ppermute x3, waiting for transfers between devices, with_halo(): lax.ppermute(tail, axis, [(i, (i + 1) % count) for i in range(ends)])  24.5 us
    another operation x3, local copies, waits for them, and re-layouts, body(): sums = lax.psum(jnp.stack(pieces), ('sector', 'op')) / total  15.2 us
    ppermute x3, starting transfers between devices, with_halo(): lax.ppermute(tail, axis, [(i, (i + 1) % count) for i in range(ends)])  12.7 us
    div x3, other arithmetic, body(): ratio_basis = latest / preconditioner  7.41 us
  transfers between devices with their start and end apart: 9, of which 9 were waited for; matrix products, arithmetic and copies ran while one was open for 0% of the time, Pallas kernels for 0%

profile of v1, /device:TPU:0, one launch (start us, length us, event | category | flops | bytes accessed | tf_op | source)
XLA Modules:
  0.0 325.8 jit_solution(13248368565301580009)
XLA Ops:
  7.2 1.7 multiply_reduce_fusion.24
  8.9 42.2 %psum.28 = f32[]{:T(128)} all-reduce(f32[]{:T(128)} %multiply_reduce_fusion.24), channel_id=1, replica_groups=mesh['sector'=16,'op'=2] {'sector','op'}, use_global_device_ids=true, to_apply=%region_1.0 | all-reduce | flops 1 | bytes 8 | tf_op jit(solution)/shard_map/psum | solution.py:40
  53.2 4.3 %collective-permute-start = (f32[1,256,256]{2,1,0:T(8,128)S(1)}, f32[1,256,256]{2,1,0:T(8,128)S(1)}, u32[]{:S(2)}, u32[]{:S(2)}) collective-permute-start(f32[1,256,256]{2,1,0:T(8,128)S(1)} %get-tuple-element.48), channel_id=1, source_target_pairs={{0,2},{2,4},{4,6},{6,8},{8,10},{10,12},{12,14},{14,16},{16,18},{18... | collective-permute-start | bytes 786440 | tf_op jit(solution)/shard_map/ppermute | solution.py:18
  58.8 8.3 %collective-permute-done = f32[1,256,256]{2,1,0:T(8,128)S(1)} collective-permute-done((f32[1,256,256]{2,1,0:T(8,128)S(1)}, f32[1,256,256]{2,1,0:T(8,128)S(1)}, u32[]{:S(2)}, u32[]{:S(2)}) %collective-permute-start) | collective-permute-done | bytes 262176 | tf_op jit(solution)/shard_map/ppermute | solution.py:18
  67.2 1.9 collective-permute-done.1
  70.5 2.0 convolution_bitcast_fusion.5
  72.5 8.2 %all-gather.7.cloned.1.call-done = f32[4,256,256]{2,1,0:T(8,128)} async-done(((f32[2,256,256]{2,1,0:T(8,128)}), f32[4,256,256]{2,1,0:T(8,128)}) %all-gather.7.cloned.1.call-update) | async-done | bytes 1048592 | tf_op jit(solution)/shard_map/all_gather | solution.py:56
  80.8 2.2 reduce_sum.277
  85.0 3.9 %stack.102 = f32[6]{0:T(128)S(1)} concatenate(f32[1]{0:T(128)} %bitcast.4, f32[1]{0:T(128)} %bitcast.5, f32[1]{0:T(128)} %bitcast.6, f32[1]{0:T(128)} %bitcast.7, f32[1]{0:T(128)} %bitcast.8, f32[1]{0:T(128)} %bitcast.9), dimensions={0} | concatenate | bytes 48 | tf_op jit(solution)/shard_map/stack | solution.py:73
  88.9 40.5 %psum.29 = f32[6]{0:T(128)S(1)} all-reduce(f32[6]{0:T(128)S(1)} %stack.102), channel_id=1, replica_groups=mesh['sector'=16,'op'=2] {'sector','op'}, use_global_device_ids=true, to_apply=%region_9.10 | all-reduce | flops 6 | bytes 48 | tf_op jit(solution)/shard_map/psum | solution.py:73
  135.7 2.0 fusion.10
  137.7 4.2 %collective-permute-start.2 = (f32[1,256,256]{2,1,0:T(8,128)S(1)}, f32[1,256,256]{2,1,0:T(8,128)S(1)}, u32[]{:S(2)}, u32[]{:S(2)}) collective-permute-start(f32[1,256,256]{2,1,0:T(8,128)S(1)} %get-tuple-element.44), channel_id=1, source_target_pairs={{0,2},{2,4},{4,6},{6,8},{8,10},{10,12},{12,14},{14,16},{16,18},{18... | collective-permute-start | bytes 786440 | tf_op jit(solution)/shard_map/ppermute | solution.py:18
  143.3 8.2 %collective-permute-done.2 = f32[1,256,256]{2,1,0:T(8,128)S(1)} collective-permute-done((f32[1,256,256]{2,1,0:T(8,128)S(1)}, f32[1,256,256]{2,1,0:T(8,128)S(1)}, u32[]{:S(2)}, u32[]{:S(2)}) %collective-permute-start.2) | collective-permute-done | bytes 262176 | tf_op jit(solution)/shard_map/ppermute | solution.py:18
  151.5 1.8 collective-permute-done.3
  154.7 1.9 convolution_bitcast_fusion.4
  156.8 8.3 %all-gather.9.cloned.1.call-done = f32[4,256,256]{2,1,0:T(8,128)} async-done(((f32[2,256,256]{2,1,0:T(8,128)}), f32[4,256,256]{2,1,0:T(8,128)}) %all-gather.9.cloned.1.call-update) | async-done | bytes 1048592 | tf_op jit(solution)/shard_map/all_gather | solution.py:56
  165.0 2.1 reduce_sum.285
  169.3 5.1 %stack.112 = f32[8]{0:T(128)S(1)} concatenate(f32[1]{0:T(128)} %bitcast.21, f32[1]{0:T(128)} %bitcast.22, f32[1]{0:T(128)} %bitcast.23, f32[1]{0:T(128)} %bitcast.24, f32[1]{0:T(128)} %bitcast.25, f32[1]{0:T(128)} %bitcast.26, f32[1]{0:T(128)} %bitcast.27, f32[1]{0:T(128)} %bitcast.28), dimensions={0} | concatenate | bytes 64 | tf_op jit(solution)/shard_map/stack | solution.py:73
  174.4 40.5 %psum.30 = f32[8]{0:T(128)S(1)} all-reduce(f32[8]{0:T(128)S(1)} %stack.112), channel_id=1, replica_groups=mesh['sector'=16,'op'=2] {'sector','op'}, use_global_device_ids=true, to_apply=%region_19.20 | all-reduce | flops 8 | bytes 64 | tf_op jit(solution)/shard_map/psum | solution.py:73
  222.0 4.2 %fusion.9 = (f32[2,256,256]{2,1,0:T(8,128)}, f32[2,256,256]{2,1,0:T(8,128)S(1)}) fusion(f32[2,256,256]{2,1,0:T(8,128)S(1)} %copy-done.1, f32[]{:T(128)S(6)} %rsqrt.14, f32[2,256,256]{2,1,0:T(8,128)S(1)} %get-tuple-element.33, f32[]{:T(128)} %bitcast.31, f32[2,256,256]{2,1,0:T(8,128)S(1)} %get-tuple-element.35, f32[]{:T(128)} %bitcast.30, ...), kind=kLoop, calls=%fused_computation.66 | loop fusion | flops 1048576 | bytes 3670032 | tf_op jit(solution)/shard_map/div | solution.py:62
  226.2 4.2 %collective-permute-start.4 = (f32[1,256,256]{2,1,0:T(8,128)S(1)}, f32[1,256,256]{2,1,0:T(8,128)S(1)}, u32[]{:S(2)}, u32[]{:S(2)}) collective-permute-start(f32[1,256,256]{2,1,0:T(8,128)S(1)} %get-tuple-element.40), channel_id=1, source_target_pairs={{0,2},{2,4},{4,6},{6,8},{8,10},{10,12},{12,14},{14,16},{16,18},{18... | collective-permute-start | bytes 786440 | tf_op jit(solution)/shard_map/ppermute | solution.py:18
  230.4 1.5 collective-permute-start.5
  231.9 8.0 %collective-permute-done.4 = f32[1,256,256]{2,1,0:T(8,128)S(1)} collective-permute-done((f32[1,256,256]{2,1,0:T(8,128)S(1)}, f32[1,256,256]{2,1,0:T(8,128)S(1)}, u32[]{:S(2)}, u32[]{:S(2)}) %collective-permute-start.4) | collective-permute-done | bytes 262176 | tf_op jit(solution)/shard_map/ppermute | solution.py:18
  239.9 1.8 collective-permute-done.5
  243.2 2.0 convolution_bitcast_fusion.3
  245.2 8.3 %all-gather.11.cloned.1.call-done = f32[4,256,256]{2,1,0:T(8,128)} async-done(((f32[2,256,256]{2,1,0:T(8,128)}), f32[4,256,256]{2,1,0:T(8,128)}) %all-gather.11.cloned.1.call-update) | async-done | bytes 1048592 | tf_op jit(solution)/shard_map/all_gather | solution.py:56
  253.5 2.2 reduce_sum.295
  257.0 1.5 multiply_reduce_fusion
  258.5 6.2 %stack.124 = f32[10]{0:T(128)S(1)} concatenate(f32[1]{0:T(128)} %bitcast.40, f32[1]{0:T(128)} %bitcast.41, f32[1]{0:T(128)} %bitcast.42, f32[1]{0:T(128)} %bitcast.43, f32[1]{0:T(128)} %bitcast.44, f32[1]{0:T(128)} %bitcast.45, f32[1]{0:T(128)} %bitcast.46, f32[1]{0:T(128)} %bitcast.47, f32[1]{0:T(128)} %bitcast.48, f32[1]{0:T(128)} %bitcast.49), dimensions={0} | concatenate | bytes 80 | tf_op jit(solution)/shard_map/stack | solution.py:73
  264.8 40.5 %psum.31 = f32[10]{0:T(128)S(1)} all-reduce(f32[10]{0:T(128)S(1)} %stack.124), channel_id=1, replica_groups=mesh['sector'=16,'op'=2] {'sector','op'}, use_global_device_ids=true, to_apply=%region_32.33 | all-reduce | flops 10 | bytes 80 | tf_op jit(solution)/shard_map/psum | solution.py:73
  307.9 2.5 pad_maximum_fusion.7
  314.8 3.5 %multiply_bitcast_fusion = f32[1,2,128,256]{3,2,1,0:T(8,128)S(1)} fusion(f32[2,256,256]{2,1,0:T(8,128)S(1)} %get-tuple-element.29, s32[]{:T(128)S(6)} %select_n.22, f32[2,256,256]{2,1,0:T(8,128)} %copy-done.14, f32[2,256,256]{2,1,0:T(8,128)S(1)} %copy-done.13, f32[2,256,256]{2,1,0:T(8,128)S(1)} %get-tuple-element.33, ...), kind=kLoop, calls=%fused_computation.27 | loop fusion | flops 589824 | bytes 1572888 | tf_op jit(solution)/shard_map/stack | solution.py:92
  (69 shorter events, 20.8 us)
Async XLA Ops:
  7.2 62.0 %copy-start = (f32[2,2,256,256]{3,2,1,0:T(8,128)S(1)}, f32[2,2,256,256]{3,2,1,0:T(8,128)}, u32[]{:S(2)}) copy-start(f32[2,2,256,256]{3,2,1,0:T(8,128)} %param.6) | copy-start | bytes 3145732
  7.2 73.6 %all-gather.7.cloned.1.call-start = ((), (), s32[]{:S(2)}) async-start(), calls=%async_computation | async-start | bytes 1572864 | tf_op jit(solution)/shard_map/all_gather | solution.py:56
  53.1 31.1 %copy-start.6 = (f32[2,256,256]{2,1,0:T(8,128)}, f32[2,256,256]{2,1,0:T(8,128)S(1)}, u32[]{:S(2)}) copy-start(f32[2,256,256]{2,1,0:T(8,128)S(1)} %get-tuple-element.34) | copy-start | bytes 1572868
  53.2 5.6 %copy-start.16 = (s32[2]{0:T(128)S(1)}, s32[2]{0:T(128)}, u32[]{:S(2)}) copy-start(s32[2]{0:T(128)} %param.8) | copy-start | bytes 28
  53.2 14.0 %collective-permute-start = (f32[1,256,256]{2,1,0:T(8,128)S(1)}, f32[1,256,256]{2,1,0:T(8,128)S(1)}, u32[]{:S(2)}, u32[]{:S(2)}) collective-permute-start(f32[1,256,256]{2,1,0:T(8,128)S(1)} %get-tuple-element.48), channel_id=1, source_target_pairs={{0,2},{2,4},{4,6},{6,8},{8,10},{10,12},{12,14},{14,16},{16,18},{18... | collective-permute-start | bytes 786440 | tf_op jit(solution)/shard_map/ppermute | solution.py:18
  57.5 11.5 %collective-permute-start.1 = (f32[1,256,256]{2,1,0:T(8,128)S(1)}, f32[1,256,256]{2,1,0:T(8,128)S(1)}, u32[]{:S(2)}, u32[]{:S(2)}) collective-permute-start(f32[1,256,256]{2,1,0:T(8,128)S(1)} %get-tuple-element.49), channel_id=1, source_target_pairs={{2,0},{4,2},{6,4},{8,6},{10,8},{12,10},{14,12},{16,14},{18,16},{20... | collective-permute-start | bytes 786440 | tf_op jit(solution)/shard_map/ppermute | solution.py:20
  69.1 1.4 copy-start.2
  72.5 92.5 %all-gather.9.cloned.1.call-start = ((), (), s32[]{:S(2)}) async-start(), calls=%async_computation.1 | async-start | bytes 1572864 | tf_op jit(solution)/shard_map/all_gather | solution.py:56
  80.8 2.2 copy-start.1
  83.0 1.2 copy-start.11
  84.2 0.9 copy-start.8
  137.7 30.7 %copy-start.5 = (f32[2,256,256]{2,1,0:T(8,128)}, f32[2,256,256]{2,1,0:T(8,128)S(1)}, u32[]{:S(2)}) copy-start(f32[2,256,256]{2,1,0:T(8,128)S(1)} %get-tuple-element.32) | copy-start | bytes 1572868
  137.7 13.7 %collective-permute-start.2 = (f32[1,256,256]{2,1,0:T(8,128)S(1)}, f32[1,256,256]{2,1,0:T(8,128)S(1)}, u32[]{:S(2)}, u32[]{:S(2)}) collective-permute-start(f32[1,256,256]{2,1,0:T(8,128)S(1)} %get-tuple-element.44), channel_id=1, source_target_pairs={{0,2},{2,4},{4,6},{6,8},{8,10},{10,12},{12,14},{14,16},{16,18},{18... | collective-permute-start | bytes 786440 | tf_op jit(solution)/shard_map/ppermute | solution.py:18
  142.0 11.3 %collective-permute-start.3 = (f32[1,256,256]{2,1,0:T(8,128)S(1)}, f32[1,256,256]{2,1,0:T(8,128)S(1)}, u32[]{:S(2)}, u32[]{:S(2)}) collective-permute-start(f32[1,256,256]{2,1,0:T(8,128)S(1)} %get-tuple-element.45), channel_id=1, source_target_pairs={{2,0},{4,2},{6,4},{8,6},{10,8},{12,10},{14,12},{16,14},{18,16},{20... | collective-permute-start | bytes 786440 | tf_op jit(solution)/shard_map/ppermute | solution.py:20
  153.4 1.4 copy-start.3
  156.7 96.8 %all-gather.11.cloned.1.call-start = ((), (), s32[]{:S(2)}) async-start(), calls=%async_computation.2 | async-start | bytes 1572864 | tf_op jit(solution)/shard_map/all_gather | solution.py:56
  167.2 1.2 copy-start.10
  168.3 0.9 copy-start.7
  226.2 13.7 %collective-permute-start.4 = (f32[1,256,256]{2,1,0:T(8,128)S(1)}, f32[1,256,256]{2,1,0:T(8,128)S(1)}, u32[]{:S(2)}, u32[]{:S(2)}) collective-permute-start(f32[1,256,256]{2,1,0:T(8,128)S(1)} %get-tuple-element.40), channel_id=1, source_target_pairs={{0,2},{2,4},{4,6},{6,8},{8,10},{10,12},{12,14},{14,16},{16,18},{18... | collective-permute-start | bytes 786440 | tf_op jit(solution)/shard_map/ppermute | solution.py:18
  230.4 11.3 %collective-permute-start.5 = (f32[1,256,256]{2,1,0:T(8,128)S(1)}, f32[1,256,256]{2,1,0:T(8,128)S(1)}, u32[]{:S(2)}, u32[]{:S(2)}) collective-permute-start(f32[1,256,256]{2,1,0:T(8,128)S(1)} %get-tuple-element.41), channel_id=1, source_target_pairs={{2,0},{4,2},{6,4},{8,6},{10,8},{12,10},{14,12},{16,14},{18,16},{20... | collective-permute-start | bytes 786440 | tf_op jit(solution)/shard_map/ppermute | solution.py:20
  241.8 1.4 copy-start.4
  255.7 1.2 copy-start.9
  255.7 1.4 copy-start.12
  256.9 1.7 copy-start.14
  257.0 57.7 %copy-start.13 = (f32[2,256,256]{2,1,0:T(8,128)S(1)}, f32[2,256,256]{2,1,0:T(8,128)}, u32[]{:S(2)}) copy-start(f32[2,256,256]{2,1,0:T(8,128)} %get-tuple-element.28) | copy-start | bytes 1572868
  314.8 3.5 %copy-start.15 = (f32[1,2,128,256]{3,2,1,0:T(8,128)S(1)}, f32[1,2,128,256]{3,2,1,0:T(8,128)}, u32[]{:S(2)}) copy-start(f32[1,2,128,256]{3,2,1,0:T(8,128)} %get-tuple-element.37) | copy-start | bytes 786436
Sparse Core Ops, SparseCore 0:
  72.6 8.1 all-gather.6
  156.8 8.1 all-gather.8
  245.3 8.1 all-gather.10
